TPU v7x, 128 devices: a whole 4x4x4 slice. The times are simulated.
128 devices in a mesh: req: 16 (over z, y), mlp: 8 (over x, core).
Axes of the slice: x: 4, y: 4, z: 4, core: 2. Of those that a mesh axis runs over, the one named last changes fastest.
Arguments:
- tokens: bfloat16 [4096, 2048], P('req', 'mlp'), may hold values from -5 to 5
- attn_gain: float32 [2048], replicated, may hold values from 0.5 to 1.5
- mlp_gain: float32 [2048], replicated, may hold values from 0.5 to 1.5
- final_gain: float32 [2048], replicated, may hold values from 0.25 to 4
- q_gain: float32 [64], replicated, may hold values from 0.5 to 1.5
- k_gain: float32 [64], replicated, may hold values from 0.25 to 4
- w_query: bfloat16 [2048, 2048], P(None, 'mlp'), may hold values from -0.125 to 0.125
- w_keyval: bfloat16 [2048, 1024], P(None, 'mlp'), may hold values from -0.125 to 0.125
- w_out: bfloat16 [2048, 2048], P('mlp'), may hold values from -0.125 to 0.125
- w_gate: bfloat16 [2048, 8192], P(None, 'mlp'), may hold values from -0.125 to 0.125
- w_up: bfloat16 [2048, 8192], P(None, 'mlp'), may hold values from -0.125 to 0.125
- w_down: bfloat16 [8192, 2048], P('mlp'), may hold values from -0.0625 to 0.0625
- w_head: bfloat16 [2048, 65536], P('req', 'mlp'), may hold values from -0.42 to 0.42
- targets: int32 [4096], P('req'), may hold values from 0 to 65535
- req_lengths: int32 [16, 4], P('req'), may hold values from 1 to 128, 256 in all within a row
- req_tenant: int32 [16, 4], P('req'), may hold values from 0 to 3
- prefix_piece: int32 [16], replicated, may hold values from 0 to 15, each once
- prefix_kv: bfloat16 [16, 1024, 1024], P('req', None, 'mlp'), may hold values from -160 to 160
Outputs:
- hidden_out: bfloat16 [4096, 2048], P('req', 'mlp')
- logprob: float32 [4096], P('req')
Inputs may be any that keep to these rules, and one draw needn't show every extreme that they name: `req_lengths`: each row sums to 256; its longest request has exactly 128 tokens. `prefix_piece`: every piece number appears once; piece n is part n % 4 of the prefix of tenant n // 4.
All inputs are finite; a program needn't handle non-finite values.
Results may differ from a plain program's by a relative error of at most 0.023.
Values may be sent and summed in bfloat16 or wider, within the bound.
A program may use at most 128 MiB of HBM per device.

v0:
```python
import math
import jax
import jax.numpy as jnp
from jax import lax
from jax.sharding import PartitionSpec as P

TENANTS = 4
PLEN = 4096
EPS = 1e-05
LOG_THETA = math.log(1000000.0)
NEG = -1e30


def rms_norm(values, gain):
    return values * lax.rsqrt(jnp.mean(values * values, axis=-1, keepdims=True) + EPS) * gain


def rope_tables(position, size):
    half = size // 2
    freq = jnp.exp(jnp.arange(half, dtype=jnp.float32) * (-2.0 * LOG_THETA / size))
    angle = position[:, None] * freq[None, :]
    return (jnp.cos(angle), jnp.sin(angle))


def rotate(values, cosine, sine):
    half = values.shape[-1] // 2
    first = values[..., :half]
    second = values[..., half:]
    cosine = cosine[:, None, :]
    sine = sine[:, None, :]
    return jnp.concatenate(
        [first * cosine - second * sine, first * sine + second * cosine], axis=-1
    )


def row_layout(lengths, tenants, count):
    ends = jnp.cumsum(lengths)
    row_ids = jnp.arange(count, dtype=jnp.int32)
    request = jnp.sum((row_ids[:, None] >= ends[None, :]).astype(jnp.int32), axis=1)
    onehot = (request[:, None] == jnp.arange(lengths.shape[0], dtype=jnp.int32)[None, :]).astype(
        jnp.int32
    )
    starts = ends - lengths
    offset = row_ids - jnp.sum(onehot * starts[None, :], axis=1)
    tenant = jnp.sum(onehot * tenants[None, :], axis=1)
    return (request, offset, tenant)


def absorb(state, queries, keys, values, seen, scale):
    best, total, accum = state
    scores = jnp.einsum("kqd,knd->kqn", queries, keys, preferred_element_type=jnp.float32) * scale
    scores = jnp.where(seen[None], scores, NEG)
    new_best = jnp.maximum(best, jnp.max(scores, axis=-1))
    keep = jnp.exp(best - new_best)
    weights = jnp.where(seen[None], jnp.exp(scores - new_best[..., None]), 0.0)
    total = total * keep + jnp.sum(weights, axis=-1)
    accum = accum * keep[..., None] + jnp.einsum(
        "kqn,knd->kqd", weights.astype(jnp.bfloat16), values, preferred_element_type=jnp.float32
    )
    return (new_best, total, accum)


def body(
    tokens,
    attn_gain,
    mlp_gain,
    final_gain,
    q_gain,
    k_gain,
    w_query,
    w_keyval,
    w_out,
    w_gate,
    w_up,
    w_down,
    w_head,
    targets,
    req_lengths,
    req_tenant,
    prefix_piece,
    prefix_kv,
):
    rows = tokens.shape[0]
    head_size = q_gain.shape[0]
    local_kv = w_keyval.shape[1] // (2 * head_size)
    local_q = w_query.shape[1] // head_size
    group = local_q // local_kv
    split_count = lax.axis_size("req") // TENANTS
    scale = head_size ** (-0.5)
    stream = lax.all_gather(tokens, "mlp", axis=1, tiled=True)
    stream_f = stream.astype(jnp.float32)
    normed = rms_norm(stream_f, attn_gain).astype(jnp.bfloat16)
    query = jnp.dot(normed, w_query, preferred_element_type=jnp.float32).reshape(
        rows, local_q, head_size
    )
    keyval = jnp.dot(normed, w_keyval, preferred_element_type=jnp.float32).reshape(
        rows, local_kv, 2, head_size
    )
    request, offset, tenant = row_layout(req_lengths[0], req_tenant[0], rows)
    cosine, sine = rope_tables((PLEN + offset).astype(jnp.float32), head_size)
    query = rotate(rms_norm(query, q_gain), cosine, sine).astype(jnp.bfloat16)
    own_keys = (
        rotate(rms_norm(keyval[:, :, 0], k_gain), cosine, sine)
        .astype(jnp.bfloat16)
        .transpose(1, 0, 2)
    )
    own_vals = keyval[:, :, 1].astype(jnp.bfloat16).transpose(1, 0, 2)
    queries = (
        query.reshape(rows, local_kv, group, head_size)
        .transpose(1, 2, 0, 3)
        .reshape(local_kv, group * rows, head_size)
    )
    start_state = (
        jnp.full((local_kv, group * rows), NEG, jnp.float32),
        jnp.zeros((local_kv, group * rows), jnp.float32),
        jnp.zeros((local_kv, group * rows, head_size), jnp.float32),
    )
    piece = lax.all_gather(prefix_kv, "req", axis=0, tiled=True)
    slab = piece.shape[1]

    def one_piece(index, inner_state):
        block = lax.dynamic_index_in_dim(piece, index, 0, keepdims=False).reshape(
            slab, local_kv, 2, head_size
        )
        block_keys = block[:, :, 0].transpose(1, 0, 2)
        block_vals = block[:, :, 1].transpose(1, 0, 2)
        owner_tenant = (
            lax.dynamic_index_in_dim(prefix_piece, index, 0, keepdims=False) // split_count
        )
        seen = jnp.tile(tenant == owner_tenant, group)[:, None]
        return absorb(inner_state, queries, block_keys, block_vals, seen, scale)

    state = lax.fori_loop(0, piece.shape[0], one_piece, start_state)
    row_ids = jnp.arange(rows, dtype=jnp.int32)
    causal = (request[:, None] == request[None, :]) & (row_ids[None, :] <= row_ids[:, None])
    best, total, accum = absorb(
        state, queries, own_keys, own_vals, jnp.tile(causal, (group, 1)), scale
    )
    attended = (
        (accum / total[..., None])
        .reshape(local_kv, group, rows, head_size)
        .transpose(2, 0, 1, 3)
        .reshape(rows, local_q * head_size)
        .astype(jnp.bfloat16)
    )
    attn_proj = jnp.dot(attended, w_out, preferred_element_type=jnp.float32)
    attn_part = lax.psum_scatter(
        attn_proj.astype(jnp.bfloat16), "mlp", scatter_dimension=1, tiled=True
    ).astype(jnp.float32)
    mid_share = (tokens.astype(jnp.float32) + attn_part).astype(jnp.bfloat16)
    middle = lax.all_gather(mid_share, "mlp", axis=1, tiled=True)
    middle_f = middle.astype(jnp.float32)
    normed_mid = rms_norm(middle_f, mlp_gain).astype(jnp.bfloat16)
    gate = jnp.dot(normed_mid, w_gate, preferred_element_type=jnp.float32)
    upper = jnp.dot(normed_mid, w_up, preferred_element_type=jnp.float32)
    inner = (jax.nn.silu(gate) * upper).astype(jnp.bfloat16)
    down = jnp.dot(inner, w_down, preferred_element_type=jnp.float32)
    down_part = lax.psum_scatter(
        down.astype(jnp.bfloat16), "mlp", scatter_dimension=1, tiled=True
    ).astype(jnp.float32)
    out_share = (mid_share.astype(jnp.float32) + down_part).astype(jnp.bfloat16)
    hidden_full = lax.all_gather(out_share, "mlp", axis=1, tiled=True)
    normed_out = rms_norm(hidden_full.astype(jnp.float32), final_gain).astype(jnp.bfloat16)
    vocab_local = w_head.shape[1]
    logits = jnp.dot(
        normed_out,
        lax.all_gather(w_head, "req", axis=0, tiled=True),
        preferred_element_type=jnp.float32,
    )
    vocab_start = lax.axis_index("mlp") * vocab_local
    top = lax.pmax(jnp.max(logits, axis=1), "mlp")
    hit = targets[:, None] - vocab_start == jnp.arange(vocab_local, dtype=jnp.int32)[None, :]
    totals, picked = lax.psum(
        (
            jnp.sum(jnp.exp(logits - top[:, None]), axis=1),
            jnp.sum(jnp.where(hit, logits, 0.0), axis=1),
        ),
        "mlp",
    )
    logprob = picked - top - jnp.log(totals)
    return (out_share, logprob)


def solution(mesh):
    in_specs = (
        P("req", "mlp"),
        P(),
        P(),
        P(),
        P(),
        P(),
        P(None, "mlp"),
        P(None, "mlp"),
        P("mlp", None),
        P(None, "mlp"),
        P(None, "mlp"),
        P("mlp", None),
        P("req", "mlp"),
        P("req"),
        P("req", None),
        P("req", None),
        P(),
        P("req", None, "mlp"),
    )
    out_specs = (P("req", "mlp"), P("req"))
    return jax.shard_map(body, mesh=mesh, in_specs=in_specs, out_specs=out_specs, check_vma=False)
```

profile of v0, /device:TPU:1, one launch (start us, length us, event | category | flops | bytes accessed | tf_op | source)
XLA Modules:
  0.0 688.8 jit_solution(6187407375356977096)
XLA Ops:
  11.8 24.9 %all-gather.8.cloned.1.call-done = bf16[256,2048]{1,0:T(8,128)(2,1)} async-done(((bf16[256,256]{1,0:T(8,128)(2,1)}), bf16[256,2048]{1,0:T(8,128)(2,1)}) %all-gather.8.cloned.1.call-update) | async-done | bytes 1048592 | tf_op jit(solution)/shard_map/all_gather | solution.py:90
  43.5 47.6 %all-gather.6.cloned.1.call-done = bf16[16,1024,128]{2,1,0:T(8,128)(2,1)} async-done(((bf16[1,1024,128]{2,1,0:T(8,128)(2,1)}), bf16[16,1024,128]{2,1,0:T(8,128)(2,1)}) %all-gather.6.cloned.1.call-update) | async-done | bytes 4194320 | tf_op jit(solution)/shard_map/all_gather | solution.py:118
  91.1 210.3 %while.20 = (s32[]{:T(128)}, f32[1,1024]{1,0:T(1,128)S(1)}, f32[1,1024]{1,0:T(1,128)S(1)}, f32[1,1024,64]{1,2,0:T(8,128)}, s32[16]{0:T(128)S(1)}, /*index=5*/s32...) while((s32[]{:T(128)}, f32[1,1024]{1,0:T(1,128)S(1)}, ...), condition=%wide.region_9.10_spmd.clone, body=%wide.region_6.0_spmd.clone.sunk | while | flops 282268928 | bytes 31530828 | solution.py:133
  95.5 2.7 fusion.94
  98.2 3.3 fusion.96
  107.7 2.7 fusion.94
  110.5 3.3 fusion.96
  123.7 3.3 fusion.96
  136.9 3.3 fusion.96
  150.1 3.3 fusion.96
  163.3 3.3 fusion.96
  176.5 3.3 fusion.96
  189.7 3.3 fusion.96
  202.9 3.3 fusion.96
  216.1 3.3 fusion.96
  229.3 3.3 fusion.96
  242.5 3.3 fusion.96
  255.7 3.3 fusion.96
  268.9 3.3 fusion.96
  282.1 3.3 fusion.96
  295.3 3.3 fusion.96
  304.6 28.8 %reduce-scatter.3.cloned.1.call-done = bf16[256,256]{1,0:T(8,128)(2,1)} async-done(((bf16[256,2048]{1,0:T(8,128)(2,1)}), bf16[256,256]{1,0:T(8,128)(2,1)}) %reduce-scatter.3.cloned.1.call-update) | async-done | bytes 131088 | tf_op jit(solution)/shard_map/reduce_scatter | solution.py:147
  335.0 25.8 %all-gather.10.cloned.1.call-done = bf16[256,2048]{1,0:T(8,128)(2,1)} async-done(((bf16[256,256]{1,0:T(8,128)(2,1)}), bf16[256,2048]{1,0:T(8,128)(2,1)}) %all-gather.10.cloned.1.call-update) | async-done | bytes 1048592 | tf_op jit(solution)/shard_map/all_gather | solution.py:151
  362.5 4.8 fusion.46
  367.3 7.3 %convolution_convert_fusion = bf16[256,2048]{1,0:T(8,128)(2,1)} fusion(bf16[1024,2048]{1,0:T(8,128)(2,1)} %param.31, bf16[2048,1024]{1,0:T(8,128)(2,1)} %param.30, f32[256,1024]{1,0:T(8,128)} %fusion.46, bf16[256,2048]{1,0:T(8,128)(2,1)S(1)} %copy-done.5, f32[2048]{0:T(1024)S(1)} %copy-done.11, f32[256]{0:T(256)S(1)} %add_rsqrt_fusion.2), kind=kOutput, calls=%fused_computation.34 | convolution fusion | flops 2151677952 | bytes 11543552 | tf_op jit(solution)/shard_map/dot_general | solution.py:157
  374.7 29.8 %reduce-scatter.5.cloned.1.call-done = bf16[256,256]{1,0:T(8,128)(2,1)} async-done(((bf16[256,2048]{1,0:T(8,128)(2,1)}), bf16[256,256]{1,0:T(8,128)(2,1)}) %reduce-scatter.5.cloned.1.call-update) | async-done | bytes 131088 | tf_op jit(solution)/shard_map/reduce_scatter | solution.py:158
  406.9 25.1 %all-gather.12.cloned.1.call-done = bf16[256,2048]{1,0:T(8,128)(2,1)} async-done(((bf16[256,256]{1,0:T(8,128)(2,1)}), bf16[256,2048]{1,0:T(8,128)(2,1)}) %all-gather.12.cloned.1.call-update) | async-done | bytes 1048592 | tf_op jit(solution)/shard_map/all_gather | solution.py:162
  433.5 198.5 %all-gather.14.cloned.1.call-done = bf16[2048,8192]{1,0:T(8,128)(2,1)} async-done(((bf16[128,8192]{1,0:T(8,128)(2,1)}), bf16[2048,8192]{1,0:T(8,128)(2,1)}) %all-gather.14.cloned.1.call-update) | async-done | bytes 33554448 | tf_op jit(solution)/shard_map/all_gather | solution.py:167
  632.0 17.4 %fusion.77 = (f32[256]{0:T(256)S(1)}, f32[256,8192]{1,0:T(8,128)}) fusion(bf16[2048,8192]{1,0:T(8,128)(2,1)} %all-gather.14.cloned.1.call-done, bf16[256,2048]{1,0:T(8,128)(2,1)} %all-gather.12.cloned.1.call-done, f32[2048]{0:T(1024)S(1)} %copy-done.12, f32[256]{0:T(256)S(1)} %add_rsqrt_fusion.1), kind=kOutput, calls=%fused_computation.123 | convolution fusion | flops 8594128896 | bytes 43001856 | tf_op jit(solution)/shard_map/dot_general | solution.py:165
  649.3 12.4 %pmax.7 = f32[256]{0:T(256)S(1)} all-reduce(f32[256]{0:T(256)S(1)} %get-tuple-element.289), channel_id=1, replica_groups=mesh['req'=16,'mlp'=8] {'mlp'}, use_global_device_ids=true, to_apply=%region_20.21 | all-reduce | flops 256 | bytes 2048 | tf_op jit(solution)/shard_map/pmax | solution.py:171
  661.8 5.1 select_reduce_fusion
  666.9 14.5 %all-reduce = (f32[256]{0:T(256)S(1)}, f32[256]{0:T(256)S(1)}) all-reduce(f32[256]{0:T(256)S(1)} %get-tuple-element.250, f32[256]{0:T(256)S(1)} %get-tuple-element.249), channel_id=1, replica_groups=mesh['req'=16,'mlp'=8] {'mlp'}, use_global_device_ids=true, to_apply=%region_22.23 | all-reduce | flops 512 | bytes 4096 | tf_op jit(solution)/shard_map/psum | solution.py:173
  (288 shorter events, 131.8 us)
Async XLA Ops:
  7.2 295.9 %copy-start = (bf16[256,2048]{1,0:T(8,128)(2,1)S(1)}, bf16[256,2048]{1,0:T(8,128)(2,1)}, u32[]{:S(2)}) copy-start(bf16[256,2048]{1,0:T(8,128)(2,1)} %param.28) | copy-start | bytes 3145732
  7.2 34.0 %copy-start.10 = (f32[2048]{0:T(1024)S(1)}, f32[2048]{0:T(1024)}, u32[]{:S(2)}) copy-start(f32[2048]{0:T(1024)} %param.21) | copy-start | bytes 24580
  7.2 33.4 %copy-start.8 = (f32[64]{0:T(128)S(1)}, f32[64]{0:T(128)}, u32[]{:S(2)}) copy-start(f32[64]{0:T(128)} %param.24) | copy-start | bytes 772
  7.2 29.5 %all-gather.8.cloned.1.call-start = ((), (), s32[]{:S(2)}) async-start(), calls=%async_computation.3 | async-start | bytes 1179648 | tf_op jit(solution)/shard_map/all_gather | solution.py:90
  7.9 83.2 %all-gather.6.cloned.1.call-start = ((), (), s32[]{:S(2)}) async-start(), calls=%async_computation.2 | async-start | bytes 4456448 | tf_op jit(solution)/shard_map/all_gather | solution.py:118
  8.7 324.7 %reduce-scatter.3.cloned.1.call-start = ((), (), s32[]{:S(2)}) async-start(), calls=%async_computation.4 | async-start | bytes 1179648 | tf_op jit(solution)/shard_map/reduce_scatter | solution.py:147
  11.8 31.1 %copy-start.9 = (f32[64]{0:T(128)S(1)}, f32[64]{0:T(128)}, u32[]{:S(2)}) copy-start(f32[64]{0:T(128)} %param.25) | copy-start | bytes 772
  36.7 4.5 copy-start.4
  38.3 52.8 %copy-start.13 = (s32[16]{0:T(128)S(1)}, s32[16]{0:T(128)}, u32[]{:S(2)}) copy-start(s32[16]{0:T(128)} %param.36) | copy-start | bytes 196
  98.2 3.4 copy-start.2
  110.5 3.4 copy-start.2
  123.7 3.4 copy-start.2
  136.9 3.4 copy-start.2
  150.1 3.4 copy-start.2
  163.3 3.4 copy-start.2
  176.5 3.4 copy-start.2
  189.7 3.4 copy-start.2
  202.9 3.4 copy-start.2
  242.5 3.4 copy-start.2
  268.9 3.4 copy-start.2
  295.3 3.4 copy-start.2
  301.4 31.9 %copy-start.6 = (bf16[256,256]{1,0:T(8,128)(2,1)S(1)}, bf16[256,256]{1,0:T(8,128)(2,1)}, u32[]{:S(2)}) copy-start(bf16[256,256]{1,0:T(8,128)(2,1)} %param.20) | copy-start | bytes 393220
  301.7 60.8 %copy-start.11 = (f32[2048]{0:T(1024)S(1)}, f32[2048]{0:T(1024)}, u32[]{:S(2)}) copy-start(f32[2048]{0:T(1024)} %param.22) | copy-start | bytes 24580
  304.6 56.3 %all-gather.10.cloned.1.call-start = ((), (), s32[]{:S(2)}) async-start(), calls=%async_computation.5 | async-start | bytes 1179648 | tf_op jit(solution)/shard_map/all_gather | solution.py:151
  335.0 69.5 %reduce-scatter.5.cloned.1.call-start = ((), (), s32[]{:S(2)}) async-start(), calls=%async_computation.6 | async-start | bytes 1179648 | tf_op jit(solution)/shard_map/reduce_scatter | solution.py:158
  360.9 6.4 copy-start.5
  367.3 37.2 %copy-start.3 = (bf16[256,256]{1,0:T(8,128)(2,1)S(1)}, bf16[256,256]{1,0:T(8,128)(2,1)}, u32[]{:S(2)}) copy-start(bf16[256,256]{1,0:T(8,128)(2,1)} %add_convert_fusion.1) | copy-start | bytes 393220
  367.3 39.6 %copy-start.7 = (s32[256]{0:T(256)S(1)}, s32[256]{0:T(256)}, u32[]{:S(2)}) copy-start(s32[256]{0:T(256)} %param.33) | copy-start | bytes 3076
  374.6 257.3 %copy-start.12 = (f32[2048]{0:T(1024)S(1)}, f32[2048]{0:T(1024)}, u32[]{:S(2)}) copy-start(f32[2048]{0:T(1024)} %param.23) | copy-start | bytes 24580
  374.7 57.3 %all-gather.12.cloned.1.call-start = ((), (), s32[]{:S(2)}) async-start(), calls=%async_computation.7 | async-start | bytes 1179648 | tf_op jit(solution)/shard_map/all_gather | solution.py:162
  406.1 225.8 %all-gather.14.cloned.1.call-start = ((), (), s32[]{:S(2)}) async-start(), calls=%async_computation.8 | async-start | bytes 35651584 | tf_op jit(solution)/shard_map/all_gather | solution.py:167
  661.8 20.2 %copy-start.1 = (bf16[256,2048]{1,0:T(8,128)(2,1)S(1)}, bf16[256,2048]{1,0:T(8,128)(2,1)}, u32[]{:S(2)}) copy-start(bf16[256,2048]{1,0:T(8,128)(2,1)} %param.28) | copy-start | bytes 3145732
  (4 other events, 13.8 us)
Sparse Core Ops, SparseCore 0:
  9.7 26.9 all-gather.7
  38.8 52.2 all-gather.5
  304.7 28.6 reduce-scatter.2
  335.5 25.3 all-gather.9
  374.8 29.6 reduce-scatter.4
  406.6 25.3 all-gather.11
  434.1 197.7 all-gather.13
where the time goes:
time: 691 us; the launch traced here: 689 us
  waiting for transfers between devices  382 us (55%)
  matrix products  122 us (18%)
  other arithmetic  70.8 us (10%)
  loops' own time  42.2 us (6%)
  local copies, waits for them, and re-layouts  29.7 us (4%)
  blocking collectives  27 us (4%)
  between operations  14.4 us (2%)
    all_gather x1, waiting for transfers between devices, body(): lax.all_gather(w_head, 'req', axis=0, tiled=True)  198 us
    reduce_sum x17, other arithmetic, absorb(): total = total * keep + jnp.sum(weights, axis=-1)  53.3 us
    all_gather x1, waiting for transfers between devices, body(): piece = lax.all_gather(prefix_kv, 'req', axis=0, tiled=True)  47.6 us
    dot_general x17, matrix products, absorb(): jnp.einsum('kqd,knd->kqn', queries, keys, preferred_element_type=jnp.floa...  43.9 us
    dot_general x17, matrix products, absorb(): jnp.einsum('kqn,knd->kqd', weights.astype(jnp.bfloat16), values, preferre...  43.1 us
    another operation x1, loops' own time, body(): state = lax.fori_loop(0, piece.shape[0], one_piece, start_state)  42.2 us
    reduce_scatter x1, waiting for transfers between devices, body(): lax.psum_scatter(down.astype(jnp.bfloat16), 'mlp', scatter_dimension=1, t...  29.8 us
    reduce_scatter x1, waiting for transfers between devices, body(): lax.psum_scatter(attn_proj.astype(jnp.bfloat16), 'mlp', scatter_dimension...  28.8 us
  transfers between devices with their start and end apart: 7, of which 7 were waited for; matrix products, arithmetic and copies ran while one was open for 2% of the time, Pallas kernels for 0%

commit v1 on v0

--- a/solution.py
+++ b/solution.py
@@ -9,6 +9,16 @@
 EPS = 1e-05
 LOG_THETA = math.log(1000000.0)
 NEG = -1e30
+
+
+def gather_by_hops(array, name, d):
+    n_dev = lax.axis_size(name)
+    block, blocks = (array, [array])
+    for _ in range(n_dev - 1):
+        block = lax.ppermute(block, name, [(i, (i + 1) % n_dev) for i in range(n_dev)])
+        blocks.insert(0, block)
+    merged = jnp.concatenate(blocks, axis=d)
+    return jnp.roll(merged, (lax.axis_index(name) + 1) * array.shape[d], axis=d)
 
 
 def rms_norm(values, gain):
@@ -87,7 +97,7 @@
     group = local_q // local_kv
     split_count = lax.axis_size("req") // TENANTS
     scale = head_size ** (-0.5)
-    stream = lax.all_gather(tokens, "mlp", axis=1, tiled=True)
+    stream = gather_by_hops(tokens, "mlp", 1)
     stream_f = stream.astype(jnp.float32)
     normed = rms_norm(stream_f, attn_gain).astype(jnp.bfloat16)
     query = jnp.dot(normed, w_query, preferred_element_type=jnp.float32).reshape(

time: 691 us -> 664 us (0.961)
  waiting for transfers between devices: 382 us -> 347 us
  starting transfers between devices: 0.46 us -> 11.2 us
    all_gather x1, waiting for transfers between devices: 47.6 us -> 15.2 us  [body(): piece = lax.all_gather(prefix_kv, 'req', axis=0, tiled=True)]
    all_gather x1 -> x0, waiting for transfers between devices: 24.9 us -> none  [body(): stream = lax.all_gather(tokens, 'mlp', axis=1, tiled=True)]
    ppermute x0 -> x7, waiting for transfers between devices: none -> 22.2 us  [gather_by_hops(): lax.ppermute(block, name, [(i, (i + 1) % n_dev) for i in range(n_dev)])]
    ppermute x0 -> x7, starting transfers between devices: none -> 10.8 us  [gather_by_hops(): lax.ppermute(block, name, [(i, (i + 1) % n_dev) for i in range(n_dev)])]
  transfers between devices with their start and end apart: 7 -> 13, of which waited for: 7 -> 13; matrix products, arithmetic and copies ran while one was open for 2% -> 1% of each run, Pallas kernels for 0% -> 0%
where the time goes in v1:
time: 664 us; the launch traced here: 662 us
  waiting for transfers between devices  347 us (52%)
  matrix products  119 us (18%)
  other arithmetic  69.4 us (10%)
  loops' own time  42.2 us (6%)
  local copies, waits for them, and re-layouts  31.3 us (5%)
  blocking collectives  27 us (4%)
  between operations  14.6 us (2%)
  starting transfers between devices  11.2 us (2%)
    all_gather x1, waiting for transfers between devices, body(): lax.all_gather(w_head, 'req', axis=0, tiled=True)  198 us
    reduce_sum x17, other arithmetic, absorb(): total = total * keep + jnp.sum(weights, axis=-1)  53.3 us
    dot_general x17, matrix products, absorb(): jnp.einsum('kqd,knd->kqn', queries, keys, preferred_element_type=jnp.floa...  44 us
    dot_general x17, matrix products, absorb(): jnp.einsum('kqn,knd->kqd', weights.astype(jnp.bfloat16), values, preferre...  43.1 us
    another operation x1, loops' own time, body(): state = lax.fori_loop(0, piece.shape[0], one_piece, start_state)  42.2 us
    reduce_scatter x1, waiting for transfers between devices, body(): lax.psum_scatter(down.astype(jnp.bfloat16), 'mlp', scatter_dimension=1, t...  29.8 us
    reduce_scatter x1, waiting for transfers between devices, body(): lax.psum_scatter(attn_proj.astype(jnp.bfloat16), 'mlp', scatter_dimension...  28.7 us
    all_gather x1, waiting for transfers between devices, body(): middle = lax.all_gather(mid_share, 'mlp', axis=1, tiled=True)  26 us
  transfers between devices with their start and end apart: 13, of which 13 were waited for; matrix products, arithmetic and copies ran while one was open for 1% of the time, Pallas kernels for 0%

profile of v1, /device:TPU:1, one launch (start us, length us, event | category | flops | bytes accessed | tf_op | source)
XLA Modules:
  0.0 661.7 jit_solution(12123885351366112311)
XLA Ops:
  24.1 3.2 collective-permute-done.3
  33.3 5.2 collective-permute-done.5
  38.7 5.4 collective-permute-done.6
  49.9 15.2 %all-gather.5.cloned.1.call-done = bf16[16,1024,128]{2,1,0:T(8,128)(2,1)} async-done(((bf16[1,1024,128]{2,1,0:T(8,128)(2,1)}), bf16[16,1024,128]{2,1,0:T(8,128)(2,1)}) %all-gather.5.cloned.1.call-update) | async-done | bytes 4194320 | tf_op jit(solution)/shard_map/all_gather | solution.py:128
  65.1 210.5 %while.20 = (s32[]{:T(128)}, f32[1,1024]{1,0:T(1,128)S(1)}, f32[1,1024]{1,0:T(1,128)S(1)}, f32[1,1024,64]{1,2,0:T(8,128)}, s32[16]{0:T(128)S(1)}, /*index=5*/s32...) while((s32[]{:T(128)}, f32[1,1024]{1,0:T(1,128)S(1)}, ...), condition=%wide.region_9.10_spmd.clone, body=%wide.region_6.9_spmd.clone.sunk | while | flops 282268928 | bytes 31530828 | solution.py:143
  72.2 3.3 fusion.98
  84.4 3.3 fusion.98
  97.7 3.3 fusion.98
  110.9 3.3 fusion.98
  124.1 3.3 fusion.98
  137.3 3.3 fusion.98
  150.5 3.3 fusion.98
  163.7 3.3 fusion.98
  176.9 3.3 fusion.98
  190.1 3.3 fusion.98
  203.4 3.3 fusion.98
  216.6 3.3 fusion.98
  229.8 3.3 fusion.98
  243.0 3.3 fusion.98
  256.2 3.3 fusion.98
  269.4 3.3 fusion.98
  278.7 28.7 %reduce-scatter.3.cloned.1.call-done = bf16[256,256]{1,0:T(8,128)(2,1)} async-done(((bf16[256,2048]{1,0:T(8,128)(2,1)}), bf16[256,256]{1,0:T(8,128)(2,1)}) %reduce-scatter.3.cloned.1.call-update) | async-done | bytes 131088 | tf_op jit(solution)/shard_map/reduce_scatter | solution.py:157
  309.1 26.0 %all-gather.7.cloned.1.call-done = bf16[256,2048]{1,0:T(8,128)(2,1)} async-done(((bf16[256,256]{1,0:T(8,128)(2,1)}), bf16[256,2048]{1,0:T(8,128)(2,1)}) %all-gather.7.cloned.1.call-update) | async-done | bytes 1048592 | tf_op jit(solution)/shard_map/all_gather | solution.py:161
  336.6 3.9 fusion.46
  340.6 7.1 %convolution_convert_fusion = bf16[256,2048]{1,0:T(8,128)(2,1)} fusion(bf16[1024,2048]{1,0:T(8,128)(2,1)} %param.31, bf16[2048,1024]{1,0:T(8,128)(2,1)} %param.30, f32[256,1024]{1,0:T(8,128)S(1)} %fusion.46, bf16[256,2048]{1,0:T(8,128)(2,1)S(1)} %copy-done.5, f32[2048]{0:T(1024)S(1)} %copy-done.13, f32[256]{0:T(256)S(1)} %add_rsqrt_fusion.2), kind=kOutput, calls=%fused_computation.34 | convolution fusion | flops 2151677952 | bytes 11543552 | tf_op jit(solution)/shard_map/dot_general | solution.py:167
  347.7 29.8 %reduce-scatter.5.cloned.1.call-done = bf16[256,256]{1,0:T(8,128)(2,1)} async-done(((bf16[256,2048]{1,0:T(8,128)(2,1)}), bf16[256,256]{1,0:T(8,128)(2,1)}) %reduce-scatter.5.cloned.1.call-update) | async-done | bytes 131088 | tf_op jit(solution)/shard_map/reduce_scatter | solution.py:168
  379.7 25.2 %all-gather.9.cloned.1.call-done = bf16[256,2048]{1,0:T(8,128)(2,1)} async-done(((bf16[256,256]{1,0:T(8,128)(2,1)}), bf16[256,2048]{1,0:T(8,128)(2,1)}) %all-gather.9.cloned.1.call-update) | async-done | bytes 1048592 | tf_op jit(solution)/shard_map/all_gather | solution.py:172
  406.5 198.3 %all-gather.11.cloned.1.call-done = bf16[2048,8192]{1,0:T(8,128)(2,1)} async-done(((bf16[128,8192]{1,0:T(8,128)(2,1)}), bf16[2048,8192]{1,0:T(8,128)(2,1)}) %all-gather.11.cloned.1.call-update) | async-done | bytes 33554448 | tf_op jit(solution)/shard_map/all_gather | solution.py:177
  604.8 17.4 %fusion.79 = (f32[256]{0:T(256)S(1)}, f32[256,8192]{1,0:T(8,128)}) fusion(bf16[2048,8192]{1,0:T(8,128)(2,1)} %all-gather.11.cloned.1.call-done, bf16[256,2048]{1,0:T(8,128)(2,1)} %all-gather.9.cloned.1.call-done, f32[2048]{0:T(1024)S(1)} %copy-done.14, f32[256]{0:T(256)S(1)} %add_rsqrt_fusion.1), kind=kOutput, calls=%fused_computation.141 | convolution fusion | flops 8594128896 | bytes 43001856 | tf_op jit(solution)/shard_map/dot_general | solution.py:175
  622.2 12.4 %pmax.7 = f32[256]{0:T(256)S(1)} all-reduce(f32[256]{0:T(256)S(1)} %get-tuple-element.289), channel_id=1, replica_groups=mesh['req'=16,'mlp'=8] {'mlp'}, use_global_device_ids=true, to_apply=%region_20.21 | all-reduce | flops 256 | bytes 2048 | tf_op jit(solution)/shard_map/pmax | solution.py:181
  634.6 5.1 select_reduce_fusion
  639.7 14.5 %all-reduce = (f32[256]{0:T(256)S(1)}, f32[256]{0:T(256)S(1)}) all-reduce(f32[256]{0:T(256)S(1)} %get-tuple-element.250, f32[256]{0:T(256)S(1)} %get-tuple-element.249), channel_id=1, replica_groups=mesh['req'=16,'mlp'=8] {'mlp'}, use_global_device_ids=true, to_apply=%region_22.23 | all-reduce | flops 512 | bytes 4096 | tf_op jit(solution)/shard_map/psum | solution.py:183
  (319 shorter events, 154.4 us)
Async XLA Ops:
  7.2 270.0 %copy-start = (bf16[256,2048]{1,0:T(8,128)(2,1)S(1)}, bf16[256,2048]{1,0:T(8,128)(2,1)}, u32[]{:S(2)}) copy-start(bf16[256,2048]{1,0:T(8,128)(2,1)} %param.28) | copy-start | bytes 3145732
  7.2 37.1 %copy-start.4 = (bf16[256,256]{1,0:T(8,128)(2,1)S(1)}, bf16[256,256]{1,0:T(8,128)(2,1)}, u32[]{:S(2)}) copy-start(bf16[256,256]{1,0:T(8,128)(2,1)} %param.20) | copy-start | bytes 393220
  7.2 57.9 %all-gather.5.cloned.1.call-start = ((), (), s32[]{:S(2)}) async-start(), calls=%async_computation.2 | async-start | bytes 4456448 | tf_op jit(solution)/shard_map/all_gather | solution.py:128
  7.9 299.5 %reduce-scatter.3.cloned.1.call-start = ((), (), s32[]{:S(2)}) async-start(), calls=%async_computation.3 | async-start | bytes 1179648 | tf_op jit(solution)/shard_map/reduce_scatter | solution.py:157
  8.0 4.9 collective-permute-start
  12.8 4.3 collective-permute-start.1
  17.1 4.5 collective-permute-start.2
  21.7 5.6 collective-permute-start.3
  27.3 5.6 collective-permute-start.4
  32.9 5.6 collective-permute-start.5
  38.5 5.6 collective-permute-start.6
  47.4 17.7 %copy-start.15 = (s32[16]{0:T(128)S(1)}, s32[16]{0:T(128)}, u32[]{:S(2)}) copy-start(s32[16]{0:T(128)} %param.36) | copy-start | bytes 196
  72.2 3.4 copy-start.2
  84.4 3.4 copy-start.2
  97.6 3.4 copy-start.2
  110.9 3.4 copy-start.2
  124.1 3.4 copy-start.2
  150.5 3.4 copy-start.2
  176.9 3.4 copy-start.2
  216.6 3.4 copy-start.2
  243.0 3.4 copy-start.2
  269.4 3.4 copy-start.2
  277.2 59.5 %copy-start.13 = (f32[2048]{0:T(1024)S(1)}, f32[2048]{0:T(1024)}, u32[]{:S(2)}) copy-start(f32[2048]{0:T(1024)} %param.22) | copy-start | bytes 24580
  278.6 56.5 %all-gather.7.cloned.1.call-start = ((), (), s32[]{:S(2)}) async-start(), calls=%async_computation.4 | async-start | bytes 1179648 | tf_op jit(solution)/shard_map/all_gather | solution.py:161
  309.1 68.4 %reduce-scatter.5.cloned.1.call-start = ((), (), s32[]{:S(2)}) async-start(), calls=%async_computation.5 | async-start | bytes 1179648 | tf_op jit(solution)/shard_map/reduce_scatter | solution.py:168
  336.6 3.9 copy-start.5
  340.5 37.0 %copy-start.3 = (bf16[256,256]{1,0:T(8,128)(2,1)S(1)}, bf16[256,256]{1,0:T(8,128)(2,1)}, u32[]{:S(2)}) copy-start(bf16[256,256]{1,0:T(8,128)(2,1)} %add_convert_fusion.1) | copy-start | bytes 393220
  347.6 32.1 %copy-start.7 = (s32[256]{0:T(256)S(1)}, s32[256]{0:T(256)}, u32[]{:S(2)}) copy-start(s32[256]{0:T(256)} %param.33) | copy-start | bytes 3076
  347.7 257.1 %copy-start.14 = (f32[2048]{0:T(1024)S(1)}, f32[2048]{0:T(1024)}, u32[]{:S(2)}) copy-start(f32[2048]{0:T(1024)} %param.23) | copy-start | bytes 24580
  347.7 57.3 %all-gather.9.cloned.1.call-start = ((), (), s32[]{:S(2)}) async-start(), calls=%async_computation.6 | async-start | bytes 1179648 | tf_op jit(solution)/shard_map/all_gather | solution.py:172
  379.1 225.7 %all-gather.11.cloned.1.call-start = ((), (), s32[]{:S(2)}) async-start(), calls=%async_computation.7 | async-start | bytes 35651584 | tf_op jit(solution)/shard_map/all_gather | solution.py:177
  634.6 20.2 %copy-start.1 = (bf16[256,2048]{1,0:T(8,128)(2,1)S(1)}, bf16[256,2048]{1,0:T(8,128)(2,1)}, u32[]{:S(2)}) copy-start(bf16[256,2048]{1,0:T(8,128)(2,1)} %param.28) | copy-start | bytes 3145732
  (12 other events, 33.0 us)
Sparse Core Ops, SparseCore 0:
  10.2 54.8 all-gather.4
  278.8 28.6 reduce-scatter.2
  309.7 25.3 all-gather.6
  347.8 29.6 reduce-scatter.4
  379.6 25.3 all-gather.8
  407.0 197.7 all-gather.10
